TPU v7x, 128 devices: a whole 4x4x4 slice. The times are simulated.
128 devices in a mesh: row: 32 (over y, z, core), col: 4 (over x).
Axes of the slice: x: 4, y: 4, z: 4, core: 2. Of those that a mesh axis runs over, the one named last changes fastest.
Arguments:
- matrix: float32 [16384, 16, 512], P('row', 'col'), may hold values from -200 to 200, as said below
Outputs:
- factored: float32 [16384, 16, 512], P('row', 'col')
- upper_rows: float32 [2, 512, 16, 512], P(None, 'row', 'col')
Inputs may be any that keep to these rules, and one draw needn't show every extreme that they name: `matrix`: Real-valued entries; every panel has full column rank.
All inputs are finite; a program needn't handle non-finite values.
Results may differ from a plain program's by a relative error of at most 0.0001.
Values sent between devices are 32-bit elements; how exact they have to be, the bound alone decides.
A program may use at most 128 MiB of HBM per device.

v0:
```python
import functools

import jax
import jax.numpy as jnp
from jax import lax
from jax.experimental import pallas as pl
from jax.experimental.pallas import tpu as pltpu
from jax.sharding import PartitionSpec as P

PANELS = 2
W = 512
SLOTS = 4
NZ = 4
NY = 4
NX = 4
PIECES = 8
LEAF = 128
NEAR_FIRST = (0, 1, 3, 2)
HIGHEST = lax.Precision.HIGHEST
MESH = pl.DeviceIdType.MESH
F32 = jnp.float32
ANY = pl.BlockSpec(memory_space=pl.ANY)


def here():
    row = lax.axis_index("row")
    x = lax.axis_index("col")
    return x, lax.div(row, 2 * NZ), lax.rem(lax.div(row, 2), NZ), lax.rem(row, 2)


def device(dx=0, dy=0, dz=0, dc=0):
    x, y, z, c = here()
    x, y, z, c = lax.rem(x + dx, NX), lax.rem(y + dy, NY), lax.rem(z + dz, NZ), lax.rem(c + dc, 2)
    return ((y * NZ + z) * 2 + c, x)


def rows(start, size):
    return pl.ds(pl.multiple_of(start, 8), size)


def greet(peers):
    for peer in peers:
        pl.semaphore_signal(pltpu.get_barrier_semaphore(), inc=1, device_id=peer, device_id_type=MESH)


class Copies:
    def __init__(self, send, recv):
        self.send, self.recv, self.used = send, recv, 0

    def make(self, src, dst, peer):
        i = self.used
        self.used += 1
        return pltpu.make_async_remote_copy(
            src_ref=src, dst_ref=dst, send_sem=self.send.at[i], recv_sem=self.recv.at[i],
            device_id=peer, device_id_type=MESH,
        )


def start(copies):
    for copy in copies:
        copy.start()


def arrive(copies):
    for copy in copies:
        copy.wait_recv()


def drain(copies):
    for copy in copies:
        copy.wait_send()


def to_others(make, buf, at, size, into, axis, me, n):
    return [
        make(buf.at[rows(at + lax.rem(me + e, n) * size, size)], into.at[e - 1], device(**{axis: e})) for e in range(1, n)
    ]


def to_all(make, buf, at, size, axis, n):
    return [make(buf.at[rows(at, size)], buf.at[rows(at, size)], device(**{axis: e})) for e in range(1, n)]


class Reduce:
    def __init__(self, make, a_buf, a_at, b_buf, b_at, size, first, second):
        x, y, z, c = here()
        q = size // 4
        self.parts = []
        for i, (buf, at, one, two) in enumerate(((a_buf, a_at, ("dz", z), ("dy", y)), (b_buf, b_at, ("dy", y), ("dz", z)))):
            mid = at + one[1] * size
            end = mid + two[1] * q
            s1 = to_others(make, buf, at, size, first.at[i], one[0], one[1], 4)
            s2 = to_others(make, buf, mid, q, second.at[i], two[0], two[1], 4)
            self.parts.append((buf, mid, size, first.at[i], s1, end, q, second.at[i], s2))

    def begin(self):
        for p in self.parts:
            start(p[4])

    def middle(self):
        for buf, mid, size, into, s1, end, q, into2, s2 in self.parts:
            arrive(s1)
            buf[rows(mid, size)] = buf[rows(mid, size)] + ((into[0] + into[1]) + into[2])
            start(s2)

    def finish(self):
        for buf, mid, size, into, s1, end, q, into2, s2 in self.parts:
            arrive(s2)
            buf[rows(end, q)] = buf[rows(end, q)] + ((into2[0] + into2[1]) + into2[2])

    def drain(self):
        for p in self.parts:
            drain(p[4])
            drain(p[8])


class AllReduce:
    def __init__(self, make, g, out, g0, g1, g2):
        x, y, z, c = here()
        half = W // 2
        q = half // 2
        a0, b0 = c * half, c * half + q
        self.g, self.out, self.g0 = g, out, g0
        self.own = rows(c * half, half)
        self.core = make(g.at[rows((1 - c) * half, half)], g0, device(dc=1))
        self.red = Reduce(make, g, a0, g, b0, q // 4, g1, g2)
        self.ends = [(p[5], p[6]) for p in self.red.parts]
        self.s1 = to_all(make, out, self.ends[0][0], q // 16, "dy", NY) + to_all(make, out, self.ends[1][0], q // 16, "dz", NZ)
        self.s2 = to_all(make, out, a0 + z * (q // 4), q // 4, "dz", NZ) + to_all(make, out, b0 + y * (q // 4), q // 4, "dy", NY)
        self.last = make(out.at[self.own], out.at[self.own], device(dc=1))

    def keep(self):
        self.red.finish()
        for at, q in self.ends:
            self.out[rows(at, q)] = self.g[rows(at, q)]

    def drain_sums(self):
        self.red.drain()
        drain([self.core])

    def drain_shares(self):
        drain([self.last] + self.s1 + self.s2)

    def step(self, i):
        if i == 0:
            self.core.start()
        elif i == 1:
            self.core.wait_recv()
            self.g[self.own] = self.g[self.own] + self.g0[...]
            self.red.begin()
        elif i == 2:
            self.red.middle()
        elif i == 3:
            self.keep()
            start(self.s1)
        elif i == 4:
            arrive(self.s1)
            start(self.s2)
        elif i == 5:
            arrive(self.s2)
            self.last.start()
        else:
            self.last.wait_recv()

    def drain(self):
        self.drain_sums()
        self.drain_shares()


class Scatter:
    def __init__(self, make, h, h0, h1, h2):
        x, y, z, c = here()
        self.h, self.h0, self.c = h, h0, c
        self.core = [make(h.at[(1 - c) * 2 + i], h0.at[i], device(dc=1)) for i in range(2)]
        self.red = Reduce(make, h.at[c * 2], 0, h.at[c * 2 + 1], 0, W // 4, h1, h2)

    def add(self, i):
        self.core[i].wait_recv()
        self.h[self.c * 2 + i] = self.h[self.c * 2 + i] + self.h0[i]

    def part(self, i):
        p = self.red.parts[i]
        return p[0][rows(p[5], p[6])]

    def drain(self):
        self.red.drain()
        drain(self.core)


class Gather:
    def __init__(self, make, wt):
        x, y, z, c = here()
        self.wt = wt
        a, b = wt.at[c * 2], wt.at[c * 2 + 1]
        self.at = ((c * 2, z * 128 + y * 32), (c * 2 + 1, y * 128 + z * 32))
        self.s1 = to_all(make, a, z * 128 + y * 32, 32, "dy", NY) + to_all(make, b, y * 128 + z * 32, 32, "dz", NZ)
        self.s2a = to_all(make, a, z * 128, 128, "dz", NZ)
        self.s2b = to_all(make, b, y * 128, 128, "dy", NY)
        self.s3a = [self.pair(make, a, lax.rem(z + NZ - e, NZ) * 128) for e in range(NZ)]
        self.s3b = [self.pair(make, b, lax.rem(y + NY - e, NY) * 128) for e in range(NY)]

    def pair(self, make, buf, at):
        return make(buf.at[rows(at, 128)], buf.at[rows(at, 128)], device(dc=1))

    def begin(self):
        start(self.s1)

    def middle(self):
        arrive(self.s1)
        start([self.s3a[0], self.s3b[0]])
        for e in (1, 3):
            start([self.s2a[e - 1], self.s2b[e - 1]])

    def far(self):
        start([self.s2a[1], self.s2b[1]])

    def forward(self):
        for e in NEAR_FIRST[1:]:
            for i in range(2):
                self.take(e, i)

    def take(self, e, i):
        arrive([(self.s2a, self.s2b)[i][e - 1]])
        start([(self.s3a, self.s3b)[i][e]])

    def back(self, e, i):
        x, y, z, c = here()
        return lax.rem((z, y)[i] + NZ - e, NZ) * 128

    def finish(self):
        arrive(self.s3a)
        arrive(self.s3b)

    def drain(self):
        drain(self.s1 + self.s2a + self.s2b + self.s3a + self.s3b)


class Relay:
    def __init__(self, make, buf, root):
        x, y, z, c = here()
        half = W // 2
        step = half // PIECES
        self.d = lax.rem(x - root + NX, NX)
        self.right = [make(buf.at[pl.ds(i * step, step)], buf.at[pl.ds(i * step, step)], device(dx=1)) for i in range(PIECES)]
        self.left = [
            make(buf.at[pl.ds(half + i * step, step)], buf.at[pl.ds(half + i * step, step)], device(dx=NX - 1))
            for i in range(PIECES)
        ]

    def begin(self):
        @pl.when(self.d == 0)
        def _():
            for a, b in zip(self.right, self.left):
                a.start()
                b.start()

    def hop(self, i):
        a, b = self.right[i], self.left[i]

        @pl.when((self.d == 1) | (self.d == 2))
        def _():
            a.wait_recv()
            a.start()

        @pl.when((self.d == 2) | (self.d == 3))
        def _():
            b.wait_recv()
            b.start()

    def finish(self):
        @pl.when(self.d == 1)
        def _():
            arrive(self.left)

        @pl.when(self.d == 3)
        def _():
            arrive(self.right)

    def drain(self):
        @pl.when(self.d != 3)
        def _():
            drain(self.right)

        @pl.when(self.d != 1)
        def _():
            drain(self.left)


def split(value):
    high = value.astype(jnp.bfloat16)
    return high, (value - high.astype(F32)).astype(jnp.bfloat16)


def dot3(a, b, dims):
    dg = functools.partial(
        lax.dot_general, dimension_numbers=(dims, ((), ())), preferred_element_type=F32
    )
    return dg(a[0], b[0]) + (dg(a[0], b[1]) + dg(a[1], b[0]))


def dot6(a, b, dims):
    return lax.dot_general(a, b, (dims, ((), ())), precision=HIGHEST, preferred_element_type=F32)


OVER_ROWS = ((0,), (0,))
OVER_COLS = ((1,), (1,))
PLAIN = ((1,), (0,))


def lanes_of(v, k):
    return jnp.broadcast_to(v[:, k : k + 1], v.shape)


def sublanes_of(v, k):
    return jnp.broadcast_to(v[k : k + 1, :], v.shape)


def leaf_inverse(slabs, zero):
    n = len(slabs)
    lane = lax.broadcasted_iota(jnp.int32, zero.shape, 1)
    sub = lax.broadcasted_iota(jnp.int32, zero.shape, 0)
    slabs = list(slabs)
    for b in range(n):
        r = slabs[b]
        inside = (lane >= 8 * b) & (lane < 8 * b + 8)
        cols = [lanes_of(r, 8 * b + s) + zero for s in range(8)]
        d = [[sublanes_of(cols[s], t) for s in range(t + 1)] for t in range(8)]
        r = jnp.where(inside, jnp.where(lane == 8 * b + sub, 1.0, 0.0), r)
        line = [sublanes_of(r, s) for s in range(8)]
        ahead = b + 1 < n
        if ahead:
            e = [lanes_of(slabs[b + 1], 8 * b + s) for s in range(8)]
            nxt = jnp.where(inside, 0.0, slabs[b + 1])
        rp = [None] * 8
        m = {}
        for s in range(8):
            rp[s] = 1.0 / d[s][s]
            if ahead:
                f = e[s] * rp[s]
                nxt = nxt - f * line[s]
                for u in range(s + 1, 8):
                    e[u] = e[u] - f * d[u][s]
            for t in range(s + 1, 8):
                m[t, s] = d[t][s] * rp[s]
            for t in range(s + 1, 8):
                for u in range(s + 1, t + 1):
                    d[t][u] = d[t][u] - m[t, s] * d[u][s]
                line[t] = line[t] - m[t, s] * line[s]
        out, pivot = line[0], d[0][0]
        for s in range(1, 8):
            out = jnp.where(sub == s, line[s], out)
            pivot = jnp.where(sub == s, d[s][s], pivot)
        slabs[b] = out * (1.0 / jnp.sqrt(pivot))
        if ahead:
            slabs[b + 1] = nxt
        if b + 2 < n:
            z = [None] * 8
            for s in reversed(range(8)):
                z[s] = line[s] * rp[s]
                for t in range(s + 1, 8):
                    z[s] = z[s] - m[t, s] * z[t]
            for i in range(b + 2, n):
                acc = jnp.where(inside, 0.0, slabs[i])
                for s in range(8):
                    acc = acc - lanes_of(slabs[i], 8 * b + s) * z[s]
                slabs[i] = acc
    return slabs


def factor(z_ref, u_ref, zero_ref, middle, end):
    w = LEAF
    ri = lax.broadcasted_iota(jnp.int32, (w, w), 0)
    ci = lax.broadcasted_iota(jnp.int32, (w, w), 1)
    wide = lax.broadcasted_iota(jnp.int32, (w, W), 1)
    down = lax.broadcasted_iota(jnp.int32, (w, W), 0)

    @pl.loop(0, W // w)
    def _(j):
        here = pl.ds(pl.multiple_of(j * w, w), w)
        block = z_ref[here, here]
        y = jnp.concatenate(leaf_inverse([block[8 * i : 8 * i + 8] for i in range(w // 8)], zero_ref[...]), axis=0)
        y = jnp.where(ci <= ri, y, 0.0)
        t = dot6(y, z_ref[here, :], PLAIN)
        u_ref[here, :] = jnp.where(wide >= j * w + down, t, 0.0)
        z_ref[here, :] = t
        z_ref[here, here] = y
        for step, do in middle.items():
            pl.when(j == step)(do)

        @pl.loop(j + 1, W // w)
        def _(i):
            there = pl.ds(pl.multiple_of(i * w, w), w)
            z_ref[there, here] = jnp.zeros((w, w), F32)
            z_ref[there, :] = z_ref[there, :] - dot6(u_ref[here, there], z_ref[here, :], OVER_ROWS)

        for step, do in end.items():
            pl.when(j == step)(do)

    @pl.loop(0, W // w)
    def _(j):
        here = pl.ds(pl.multiple_of(j * w, w), w)
        z_ref[here, :] = jnp.where(wide <= j * w + down, z_ref[here, :], 0.0)


def kernel(scale, x_ref, x_out, r_out, xs, p0, p1, pn, q0, q1, w01, z0, z1, u0, u1, zero, g, gf, g0, g1, g2,
           h, h0, h1, h2, wt, up, fix, ha, hb, send, recv, local):
    x, y, z, c = here()
    make = Copies(send, recv).make
    other = 1 - c
    loads = [pltpu.make_async_copy(x_ref.at[:, j, :], xs.at[j], local.at[j]) for j in range(SLOTS)]
    seeds = [pltpu.make_async_copy(x_ref.at[:, 0, :], p, local.at[SLOTS]) for p in (p0, p1)]
    for k in range(PANELS):
        @pl.when(x == k)
        def _():
            seeds[k].start()
    start(loads)
    zero[...] = jnp.zeros_like(zero)
    relay = [Relay(make, p, k) for k, p in enumerate((p0, p1))]
    whole = [AllReduce(make, g.at[i], gf.at[i], g0.at[i], g1.at[i], g2.at[i]) for i in range(3)]
    scatter = [Scatter(make, h, h0.at[k], h1.at[k], h2.at[k]) for k in range(PANELS)]
    gather = [Gather(make, wt.at[k]) for k in range(PANELS)]
    peers = [device(dc=1)] + [device(dz=d) for d in range(1, NZ)] + [device(dy=d) for d in range(1, NY)]
    peers += [device(dx=d) for d in range(1, NX)]
    greet(peers)

    @pl.when(x == 0)
    def _():
        seeds[0].wait()
        g[0] = dot6(p0[...], p0[...], OVER_ROWS)

    @pl.when(x == 1)
    def _():
        seeds[1].wait()

    pl.semaphore_wait(pltpu.get_barrier_semaphore(), len(peers))
    relay[0].begin()
    across = [
        [make(gf.at[0, rows(at, q)], gf.at[0, rows(at, q)], device(dx=e)) for at, q in whole[0].ends] for e in range(1, NX)
    ]

    @pl.when(x == 0)
    def _():
        for i in range(3):
            whole[0].step(i)
        whole[0].keep()
        for copies in across:
            start(copies)

    for i in range(PIECES):
        relay[0].hop(i)
    relay[1].begin()
    for e in range(1, NX):
        @pl.when(x == e)
        def _():
            arrive(across[e - 1])

    start(whole[0].s1)

    @pl.when(x != 3)
    def _():
        for i in range(2):
            relay[1].hop(i)

    relay[0].finish()
    for load in loads:
        load.wait()

    def hops(*pieces):
        for i in pieces:
            relay[1].hop(i)

    def terms(panel, steps):
        ha[0], ha[1] = split(panel[...])

        @pl.loop(0, SLOTS)
        def _(i):
            j = lax.rem(other * 2 + i, SLOTS)
            h[j] = dot3(split(xs[j]), (ha[0], ha[1]), OVER_ROWS)
            for step, do in enumerate(steps):
                pl.when(i == step)(do)

    def zero_first():
        scatter[0].core[0].start()
        whole[0].step(4)

        @pl.when(x == 3)
        def _():
            hops(0, 1)

        hops(2, 3)

    def zero_second():
        scatter[0].core[1].start()
        hops(4)
        whole[0].step(5)
        hops(5)

    terms(p0, (zero_first, zero_second, lambda: hops(6), lambda: hops(7)))
    for i in range(2):
        scatter[0].add(i)
    scatter[0].red.begin()
    whole[0].step(6)
    z0[...] = gf[0]

    def cross():
        relay[1].finish()
        g[1] = dot6(p0[...], p1[...], OVER_ROWS)
        whole[1].step(0)

    factor(
        z0, u0, zero, {0: cross, 2: lambda: whole[1].step(3), 3: lambda: whole[1].step(4)},
        {0: lambda: whole[1].step(1), 1: lambda: whole[1].step(2), 2: scatter[0].red.middle},
    )
    scatter[0].red.finish()
    inverse = z0[...]

    def shards(k, parts, inv):
        both = dot6(jnp.concatenate(parts, axis=0), inv, OVER_COLS)
        for i, (slot, at) in enumerate(gather[k].at):
            wt[k, slot, rows(at, 32)] = both[32 * i : 32 * i + 32]

    shards(0, [scatter[0].part(i) for i in range(2)], inverse)
    gather[0].begin()
    q0[...] = dot6(p0[...], inverse, OVER_COLS)
    hb[0], hb[1] = split(q0[...])
    whole[1].step(5)
    whole[1].step(6)
    w01[...] = dot6(inverse, gf[1], PLAIN)
    gather[0].middle()
    gather[0].far()

    pn[...] = p1[...] - dot6(q0[...], w01[...], PLAIN)
    g[2] = dot6(pn[...], pn[...], OVER_ROWS)
    whole[2].step(0)

    row = (y * NZ + z) * 2 + c
    mine = rows(row * 16, 16)
    pick = jnp.where(
        lax.broadcasted_iota(jnp.int32, (16, W), 1) == row * 16 + lax.broadcasted_iota(jnp.int32, (16, W), 0), 1.0, 0.0
    ).astype(F32)

    scatter[0].drain()

    def one_first():
        scatter[1].core[0].start()
        whole[2].step(1)

    terms(p1, (one_first, scatter[1].core[1].start, lambda: whole[2].step(2), lambda: whole[2].step(3)))
    gather[0].forward()
    for i in range(2):
        scatter[1].add(i)
    both = dot6(jnp.concatenate([wt[0, slot, rows(at, 32)] for slot, at in gather[0].at], axis=0), w01[...], PLAIN)
    for i in range(2):
        fix[i] = both[32 * i : 32 * i + 32]
    whole[2].step(4)
    whole[2].step(5)
    scatter[1].red.begin()
    whole[2].step(6)
    z1[...] = gf[2]
    factor(z1, u1, zero, {2: scatter[1].red.middle}, {})
    scatter[1].red.finish()
    inverse = z1[...]
    shards(1, [scatter[1].part(i) - fix[i] for i in range(2)], inverse)
    gather[1].begin()
    q1[...] = dot6(pn[...], inverse, OVER_COLS)
    ha[0], ha[1] = split(q1[...])
    gather[0].finish()
    gather[1].middle()
    gather[1].far()

    @pl.loop(0, SLOTS)
    def _(j):
        w = wt[0, j]
        new = xs[j] - dot3((hb[0], hb[1]), split(w), OVER_COLS)
        owner = (j == 0) & (x == 0)
        xs[j] = jnp.where(owner, q0[...] * scale, new)
        up[0, j] = jnp.where(owner, u0[mine], dot6(pick, w, OVER_COLS))

    def blocks(n):
        turn = lax.div(n, 2)
        e = turn + jnp.where(turn == 2, 1, 0) - jnp.where(turn == 3, 1, 0)
        slot = lax.rem(c + lax.rem(n, 2), 2) * 2
        return [(slot + i, pl.ds(pl.multiple_of(gather[1].back(e, i), 128), 128)) for i in range(2)]

    def ready(n):
        e = NEAR_FIRST[n // 2]
        if n % 2:
            arrive([gather[1].s3a[e], gather[1].s3b[e]])
        elif e:
            gather[1].take(e, 0)
            gather[1].take(e, 1)

    def store(n, i, j, lanes):
        return pltpu.make_async_copy(xs.at[j, :, lanes], x_out.at[:, j, lanes], local.at[SLOTS + 1 + 2 * n + i])

    @pl.loop(0, 2 * NZ)
    def _(n):
        for step in range(2 * NZ):
            pl.when(n == step)(functools.partial(ready, step))
        pair = blocks(n)
        w = jnp.concatenate([wt[1, j, lanes] for j, lanes in pair], axis=0)
        product = dot3((ha[0], ha[1]), split(w), OVER_COLS)
        line = dot6(pick, w, OVER_COLS)
        for i, (j, lanes) in enumerate(pair):
            own = slice(128 * i, 128 * i + 128)
            old = xs[j, :, lanes]
            skip = (j == 0) & (x < 1)
            owner = (j == 0) & (x == 1)
            xs[j, :, lanes] = jnp.where(skip, old, jnp.where(owner, q1[:, lanes] * scale, old - product[:, own]))
            up[1, j, :, lanes] = jnp.where(skip, 0.0, jnp.where(owner, u1[mine, lanes], line[:, own]))
            store(n, i, j, lanes).start()

    stores = []

    def keep(source, target):
        stores.append(pltpu.make_async_copy(source, target, local.at[SLOTS + 1 + 4 * NZ + len(stores)]))
        stores[-1].start()

    for k in range(PANELS):
        for j in range(SLOTS):
            keep(up.at[k, j], r_out.at[k, :, j, :])
    for each in stores:
        each.wait()

    @pl.loop(0, 2 * NZ)
    def _(n):
        for i, (j, lanes) in enumerate(blocks(n)):
            store(n, i, j, lanes).wait()

    for k in range(PANELS):
        relay[k].drain()
        gather[k].drain()

    @pl.when(x == 0)
    def _():
        whole[0].drain_sums()
        for copies in across:
            drain(copies)

    whole[0].drain_shares()
    whole[1].drain()
    whole[2].drain()
    scatter[1].drain()


def on_device(matrix):
    n = matrix.shape[0]
    scale = float(n * lax.axis_size("row")) ** 0.5
    dma = pltpu.SemaphoreType.DMA

    def vmem(*dims):
        return pltpu.VMEM(dims, F32)

    share = W // lax.axis_size("row")
    square = vmem(W, W)
    return pl.pallas_call(
        functools.partial(kernel, scale),
        out_shape=(
            jax.ShapeDtypeStruct((n, SLOTS, W), F32), jax.ShapeDtypeStruct((PANELS, share, SLOTS, W), F32),
        ),
        in_specs=[ANY],
        out_specs=(ANY, ANY),
        scratch_shapes=[
            vmem(SLOTS, n, W), vmem(n, W), vmem(n, W), vmem(n, W), vmem(n, W), vmem(n, W), square, square, square, square,
            square, vmem(8, LEAF), vmem(3, W, W), vmem(3, W, W), vmem(3, W // 2, W), vmem(3, 2, 3, 32, W), vmem(3, 2, 3, 8, W),
            vmem(SLOTS, W, W), vmem(2, 2, W, W), vmem(2, 2, 3, 128, W), vmem(2, 2, 3, 32, W), vmem(2, SLOTS, W, W),
            vmem(PANELS, SLOTS, share, W), vmem(2, 32, W), pltpu.VMEM((2, W, W), jnp.bfloat16),
            pltpu.VMEM((2, W, W), jnp.bfloat16), dma((208,)), dma((208,)), dma((32,)),
        ],
        compiler_params=pltpu.CompilerParams(
            collective_id=1, has_side_effects=True, vmem_limit_bytes=63 * 2**20
        ),
        name="qr",
    )(matrix)


def solution(mesh):
    return jax.shard_map(
        on_device,
        mesh=mesh,
        in_specs=(P("row", "col", None),),
        out_specs=(P("row", "col", None), P(None, "row", "col", None)),
        check_vma=False,
    )
```

profile of v0, /device:TPU:1, one launch (start us, length us, event | category | flops | bytes accessed | tf_op | source)
XLA Modules:
  0.0 160.2 jit_solution(6850175856293165713)
XLA Ops:
  0.6 153.9 %qr.1 = (f32[512,4,512]{2,1,0:T(4,128)}, f32[2,16,4,512]{3,2,1,0:T(4,128)}) custom-call(f32[512,4,512]{2,1,0:T(4,128)} %x_ref.1), custom_call_target="tpu_custom_call" | custom-call | tf_op jit(solution)/shard_map/qr/pallas_call | solution.py:656
  154.5 0.0 copy-start
  154.5 5.0 %copy.5 = f32[512,4,512]{2,1,0:T(4,128)} copy(f32[512,4,512]{2,1,0:T(4,128)} %get-tuple-element.4) | data formatting | bytes 8388608
  159.5 0.0 copy-done
  159.5 0.7 copy.6
Async XLA Ops:
  154.5 5.0 %copy-start = (f32[2,16,4,512]{3,2,1,0:T(4,128)S(1)}, f32[2,16,4,512]{3,2,1,0:T(4,128)}, u32[]{:S(2)}) copy-start(f32[2,16,4,512]{3,2,1,0:T(4,128)} %get-tuple-element.5) | copy-start | bytes 786436
where the time goes:
time: 160 us
  Pallas kernels  154 us (96%)
  local copies, waits for them, and re-layouts  5.67 us (4%)
    pallas_call x1, Pallas kernels, on_device(): pl.pallas_call(functools.partial(kernel, scale), out_shape=(jax.ShapeDtyp...  154 us
    unnamed x4, local copies, waits for them, and re-layouts  5.67 us

commit v1 on v0

--- a/solution.py
+++ b/solution.py
@@ -470,12 +470,12 @@
             relay[1].hop(i)
 
     def terms(panel, steps):
-        ha[0], ha[1] = split(panel[...])
+        ha[0, :W], ha[1, :W] = split(panel[...])
 
         @pl.loop(0, SLOTS)
         def _(i):
             j = lax.rem(other * 2 + i, SLOTS)
-            h[j] = dot3(split(xs[j]), (ha[0], ha[1]), OVER_ROWS)
+            h[j] = dot3(split(xs[j]), (ha[0, :W], ha[1, :W]), OVER_ROWS)
             for step, do in enumerate(steps):
                 pl.when(i == step)(do)
 
@@ -522,7 +522,7 @@
     shards(0, [scatter[0].part(i) for i in range(2)], inverse)
     gather[0].begin()
     q0[...] = dot6(p0[...], inverse, OVER_COLS)
-    hb[0], hb[1] = split(q0[...])
+    hb[0, :W], hb[1, :W] = split(q0[...])
     whole[1].step(5)
     whole[1].step(6)
     w01[...] = dot6(inverse, gf[1], PLAIN)
@@ -537,7 +537,10 @@
     mine = rows(row * 16, 16)
     pick = jnp.where(
         lax.broadcasted_iota(jnp.int32, (16, W), 1) == row * 16 + lax.broadcasted_iota(jnp.int32, (16, W), 0), 1.0, 0.0
-    ).astype(F32)
+    )
+    for each in (ha, hb):
+        each[0, W:] = pick.astype(jnp.bfloat16)
+        each[1, W:] = jnp.zeros(pick.shape, jnp.bfloat16)
 
     scatter[0].drain()
 
@@ -563,7 +566,7 @@
     shards(1, [scatter[1].part(i) - fix[i] for i in range(2)], inverse)
     gather[1].begin()
     q1[...] = dot6(pn[...], inverse, OVER_COLS)
-    ha[0], ha[1] = split(q1[...])
+    ha[0, :W], ha[1, :W] = split(q1[...])
     gather[0].finish()
     gather[1].middle()
     gather[1].far()
@@ -571,10 +574,10 @@
     @pl.loop(0, SLOTS)
     def _(j):
         w = wt[0, j]
-        new = xs[j] - dot3((hb[0], hb[1]), split(w), OVER_COLS)
+        product = dot3((hb[0], hb[1]), split(w), OVER_COLS)
         owner = (j == 0) & (x == 0)
-        xs[j] = jnp.where(owner, q0[...] * scale, new)
-        up[0, j] = jnp.where(owner, u0[mine], dot6(pick, w, OVER_COLS))
+        xs[j] = jnp.where(owner, q0[...] * scale, xs[j] - product[:W])
+        up[0, j] = jnp.where(owner, u0[mine], product[W:])
 
     def blocks(n):
         turn = lax.div(n, 2)
@@ -600,14 +603,13 @@
         pair = blocks(n)
         w = jnp.concatenate([wt[1, j, lanes] for j, lanes in pair], axis=0)
         product = dot3((ha[0], ha[1]), split(w), OVER_COLS)
-        line = dot6(pick, w, OVER_COLS)
         for i, (j, lanes) in enumerate(pair):
             own = slice(128 * i, 128 * i + 128)
             old = xs[j, :, lanes]
             skip = (j == 0) & (x < 1)
             owner = (j == 0) & (x == 1)
-            xs[j, :, lanes] = jnp.where(skip, old, jnp.where(owner, q1[:, lanes] * scale, old - product[:, own]))
-            up[1, j, :, lanes] = jnp.where(skip, 0.0, jnp.where(owner, u1[mine, lanes], line[:, own]))
+            xs[j, :, lanes] = jnp.where(skip, old, jnp.where(owner, q1[:, lanes] * scale, old - product[:W, own]))
+            up[1, j, :, lanes] = jnp.where(skip, 0.0, jnp.where(owner, u1[mine, lanes], product[W:, own]))
             store(n, i, j, lanes).start()
 
     stores = []
@@ -664,8 +666,8 @@
             vmem(SLOTS, n, W), vmem(n, W), vmem(n, W), vmem(n, W), vmem(n, W), vmem(n, W), square, square, square, square,
             square, vmem(8, LEAF), vmem(3, W, W), vmem(3, W, W), vmem(3, W // 2, W), vmem(3, 2, 3, 32, W), vmem(3, 2, 3, 8, W),
             vmem(SLOTS, W, W), vmem(2, 2, W, W), vmem(2, 2, 3, 128, W), vmem(2, 2, 3, 32, W), vmem(2, SLOTS, W, W),
-            vmem(PANELS, SLOTS, share, W), vmem(2, 32, W), pltpu.VMEM((2, W, W), jnp.bfloat16),
-            pltpu.VMEM((2, W, W), jnp.bfloat16), dma((208,)), dma((208,)), dma((32,)),
+            vmem(PANELS, SLOTS, share, W), vmem(2, 32, W), pltpu.VMEM((2, W + share, W), jnp.bfloat16),
+            pltpu.VMEM((2, W + share, W), jnp.bfloat16), dma((208,)), dma((208,)), dma((32,)),
         ],
         compiler_params=pltpu.CompilerParams(
             collective_id=1, has_side_effects=True, vmem_limit_bytes=63 * 2**20

time: 160 us -> 159 us (level)
  no operation moved by 1% of the time
where the time goes in v1:
time: 159 us
  Pallas kernels  153 us (96%)
  local copies, waits for them, and re-layouts  5.67 us (4%)
    pallas_call x1, Pallas kernels, on_device(): pl.pallas_call(functools.partial(kernel, scale), out_shape=(jax.ShapeDtyp...  153 us
    unnamed x4, local copies, waits for them, and re-layouts  5.67 us

profile of v1, /device:TPU:1, one launch (start us, length us, event | category | flops | bytes accessed | tf_op | source)
XLA Modules:
  0.0 159.0 jit_solution(11765597750246587862)
XLA Ops:
  0.6 152.7 %qr.1 = (f32[512,4,512]{2,1,0:T(4,128)}, f32[2,16,4,512]{3,2,1,0:T(4,128)}) custom-call(f32[512,4,512]{2,1,0:T(4,128)} %x_ref.1), custom_call_target="tpu_custom_call" | custom-call | tf_op jit(solution)/shard_map/qr/pallas_call | solution.py:658
  153.4 0.0 copy-start
  153.4 5.0 %copy.5 = f32[512,4,512]{2,1,0:T(4,128)} copy(f32[512,4,512]{2,1,0:T(4,128)} %get-tuple-element.4) | data formatting | bytes 8388608
  158.3 0.0 copy-done
  158.3 0.7 copy.6
Async XLA Ops:
  153.4 5.0 %copy-start = (f32[2,16,4,512]{3,2,1,0:T(4,128)S(1)}, f32[2,16,4,512]{3,2,1,0:T(4,128)}, u32[]{:S(2)}) copy-start(f32[2,16,4,512]{3,2,1,0:T(4,128)} %get-tuple-element.5) | copy-start | bytes 786436
